TPU v7x, 32 devices: a whole 2x2x4 slice. The times are simulated.
32 devices in a mesh: band: 4 (over y, x), slab: 8 (over z, core).
Axes of the slice: x: 2, y: 2, z: 4, core: 2. Of those that a mesh axis runs over, the one named last changes fastest.
Arguments:
- coefficients: float32 [8, 96, 96, 192], P('band', 'slab'), may hold values from -6 to 6
- occupation: int32 [8], P('band'), may hold values from 1 to 2
- pencil_reach: int32 [96, 96], P('slab'), may hold values from -1 to 47
- external: float32 [192, 192, 192], P(None, 'slab'), may hold values from -3 to 3
Outputs:
- applied: float32 [8, 96, 96, 192], P('band', 'slab')
- potential: float32 [192, 192, 192], P(None, 'slab')
All inputs are finite; a program needn't handle non-finite values.
Results may differ from a plain program's by a relative error of at most 0.00011.
Values sent between devices are 32-bit elements; how exact they have to be, the bound alone decides.
A program may use at most 128 MiB of HBM per device.

v0:
```python
import math

import jax
import jax.numpy as jnp
from jax import lax
from jax.sharding import PartitionSpec as P

KINETIC = 0.0005
SLATER = 0.9847


def frequency(length):
    indices = jnp.arange(length, dtype=jnp.int32)
    return jnp.where(indices < length // 2, indices, indices - length)


def inverse_table(length, extent):
    wavenumbers = frequency(length)
    positions = jnp.arange(extent, dtype=jnp.int32)
    phases = positions[:, None] * wavenumbers[None, :] % extent
    angles = phases.astype(jnp.float32) * (2.0 * math.pi / extent)
    factor = length ** (-0.5)
    cosine = jnp.cos(angles) * factor
    sine_part = jnp.sin(angles) * factor
    return jnp.stack([jnp.stack([cosine, -sine_part], 1), jnp.stack([sine_part, cosine], 1)], 0)


def forward_table(length, extent):
    wavenumbers = frequency(length)
    positions = jnp.arange(extent, dtype=jnp.int32)
    phases = wavenumbers[:, None] * positions[None, :] % extent
    angles = phases.astype(jnp.float32) * (2.0 * math.pi / extent)
    factor = length**0.5 / extent
    cosine = jnp.cos(angles) * factor
    sine_part = jnp.sin(angles) * factor
    return jnp.stack([jnp.stack([cosine, sine_part], 1), jnp.stack([-sine_part, cosine], 1)], 0)


def contract(form, left, right):
    return jnp.einsum(form, left, right, precision=lax.Precision.HIGHEST)


def shards(coefficients, occupation, pencil_reach, external):
    nbands, planes, width, doubled = coefficients.shape
    points = 2 * width
    slabs = lax.axis_size("slab")
    layers = points // slabs
    groups = lax.axis_size("band")
    inverse = inverse_table(width, points)
    forward = forward_table(width, points)
    wavenumbers = frequency(width)
    sphere = (jnp.abs(wavenumbers)[None, None, :] <= pencil_reach[:, :, None]).astype(jnp.float32)
    sphere_full = sphere[None, :, :, None, :]
    masked = coefficients.reshape(nbands, planes, width, 2, width) * sphere_full
    along_z = contract("bxgci,onci->bxnog", masked, inverse)
    flattened = along_z.reshape(nbands, planes, points, 2 * width)
    received = lax.all_to_all(flattened, "slab", split_axis=2, concat_axis=1, tiled=True)
    columns = received.reshape(received.shape[0], width, layers, 2, width)
    spread = contract("bkzcg,oycg->bkzoy", columns, inverse)
    wavefield = contract("bkzcy,oxck->bxzoy", spread, inverse)
    squares = jnp.sum(wavefield * wavefield, axis=3)
    weights = occupation.astype(jnp.float32) / (nbands * groups)
    partial_value = contract("b,bxzy->xzy", weights, squares)
    rows_all = points * layers
    share = (rows_all + groups - 1) // groups
    flat_partial = partial_value.reshape(rows_all, points)
    density = lax.psum_scatter(flat_partial, "band", scatter_dimension=0, tiled=True)
    flat_external = external.reshape(rows_all, points)
    start_row = lax.axis_index("band") * share
    own_external = lax.dynamic_slice_in_dim(flat_external, start_row, share, 0)
    own_potential = own_external - SLATER * jnp.cbrt(density)
    gathered = lax.all_gather(own_potential, "band", axis=0, tiled=True)
    potential_all = gathered.reshape(points, layers, points)
    product = wavefield * potential_all[None, :, :, None, :]
    back_rows = contract("bxzcy,okcx->bkzoy", product, forward)
    back_y = contract("bkzcy,ogcy->bkzog", back_rows, forward).reshape(
        nbands, width, layers, 2 * width
    )
    received = lax.all_to_all(back_y, "slab", split_axis=1, concat_axis=2, tiled=True)
    blocks = received.reshape(received.shape[0], planes, points, 2, width)
    returned = contract("bxncg,ohcn->bxgoh", blocks, forward)
    plane_index = lax.axis_index("slab") * planes + jnp.arange(planes, dtype=jnp.int32)
    plane_freq = jnp.where(plane_index < width // 2, plane_index, plane_index - width)
    plane_sq = (plane_freq * plane_freq).astype(jnp.float32)
    wave_sq = (wavenumbers * wavenumbers).astype(jnp.float32)
    kinetic = KINETIC * (plane_sq[:, None, None] + wave_sq[None, :, None] + wave_sq[None, None, :])
    finished = sphere_full * (kinetic[None, :, :, None, :] * masked + returned)
    return (finished.reshape(nbands, planes, width, 2 * width), potential_all)


def solution(mesh):
    return jax.shard_map(
        shards,
        mesh=mesh,
        in_specs=(P("band", "slab", None, None), P("band"), P("slab", None), P(None, "slab", None)),
        out_specs=(P("band", "slab", None, None), P(None, "slab", None)),
        check_vma=False,
    )
```

profile of v0, /device:TPU:0, one launch (start us, length us, event | category | flops | bytes accessed | tf_op | source)
XLA Modules:
  0.0 507.4 jit_solution(4915318671255443394)
XLA Ops:
  7.2 0.4 fusion.44
  7.6 0.0 copy-start.6
  7.6 3.2 copy.51
  10.8 2.0 copy.52
  12.8 0.0 copy-done.6
  12.8 0.0 copy-start
  12.9 0.2 compare_convert_fusion
  13.1 0.0 copy-start.2
  13.1 1.0 copy-done.2
  14.1 3.9 fusion.20
  18.0 2.7 copy.53
  20.7 0.0 copy-done
  20.7 7.9 %copy.54 = f32[2,12,192,192]{3,0,1,2:T(2,128)} copy(f32[2,12,192,192]{2,3,1,0:T(8,128)} %bitcast.112) | data formatting | bytes 7077888 | tf_op jit(solution)/shard_map/reshape | solution.py:56
  28.7 0.0 copy-start.7
  28.7 6.5 %all-to-all-start = ((f32[2,12,192,192]{3,0,1,2:T(2,128)}), f32[2,12,192,192]{3,0,1,2:T(2,128)}, u32[]{:S(2)}, u32[]{:S(2)}) async-start(f32[2,12,192,192]{3,0,1,2:T(2,128)} %copy.54), calls=%async_computation | async-start | bytes 9437184 | tf_op jit(solution)/shard_map/all_to_all | solution.py:57
  35.2 0.2 reduce-scatter.2.cloned.1.call-start
  35.4 0.0 copy-done.7
  35.4 105.1 %all-to-all-done = f32[2,12,192,192]{3,0,1,2:T(2,128)} async-done(((f32[2,12,192,192]{3,0,1,2:T(2,128)}), f32[2,12,192,192]{3,0,1,2:T(2,128)}, u32[]{:S(2)}, u32[]{:S(2)}) %all-to-all-start) | async-done | bytes 3538976 | tf_op jit(solution)/shard_map/all_to_all | solution.py:57
  140.5 3.9 copy.55
  144.3 2.7 copy.56
  147.0 7.1 %reshape.334 = f32[2,96,24,2,96]{4,3,2,1,0:T(2,128)} reshape(f32[2,8,12,24,192]{4,3,2,1,0:T(8,128)} %copy.56) | data formatting | bytes 7077888 | tf_op jit(solution)/shard_map/reshape | solution.py:58
  154.2 11.6 %fusion.12 = f32[2,96,24,2,192,1]{4,1,5,3,2,0:T(8,128)S(1)} fusion(f32[2,96,24,2,96,1]{4,3,2,1,0,5:T(2,128)} %bitcast.108, f32[1,192,2,96]{3,1,2,0:T(8,128)S(1)} %get-tuple-element.13, f32[1,192,2,96]{3,1,2,0:T(8,128)S(1)} %get-tuple-element.12), kind=kOutput, calls=%fused_computation.15 | convolution fusion | flops 4076937216 | bytes 10911744 | tf_op jit(solution)/shard_map/bkzcg,oycg->bkzoy/dot_general | solution.py:40
  165.8 22.2 %fusion.2 = (f32[192,2,24,192]{3,0,2,1:T(8,128)S(1)}, f32[2,192,2,24,192,1]{4,1,5,3,2,0:T(8,128)}) fusion(f32[2,96,24,2,192,1]{4,1,5,3,2,0:T(8,128)S(1)} %fusion.12, f32[1,192,2,96]{3,1,2,0:T(8,128)S(1)} %get-tuple-element.13, f32[1,192,2,96]{3,1,2,0:T(8,128)S(1)} %get-tuple-element.12), kind=kOutput, calls=%fused_computation.4 | convolution fusion | flops 8159109120 | bytes 28606464 | tf_op jit(solution)/shard_map/bkzcy,oxck->bxzoy/dot_general | solution.py:40
  187.9 5.5 %copy.58 = f32[192,24,192,2]{2,1,0,3:T(8,128)S(1)} copy(f32[192,24,192,2]{2,0,1,3:T(8,128)S(1)} %bitcast.107) | data formatting | bytes 14155776 | tf_op jit(solution)/shard_map/b,bxzy->xzy/dot_general | solution.py:40
  193.4 4.5 fusion.7
  197.9 0.0 reduce-scatter.2.cloned.1.call-update
  197.9 0.0 all-gather.2.cloned.1.call-start
  197.9 56.0 %reduce-scatter.2.cloned.1.call-done = f32[1152,192]{1,0:T(8,128)} async-done(((f32[4608,192]{1,0:T(8,128)}), f32[1152,192]{1,0:T(8,128)}) %reduce-scatter.2.cloned.1.call-update) | async-done | bytes 884752 | tf_op jit(solution)/shard_map/reduce_scatter | solution.py:67
  254.0 3.6 multiply_subtract_fusion
  257.6 0.0 all-gather.2.cloned.1.call-update
  257.6 0.5 sine_multiply_fusion.1
  258.1 0.0 copy-start.4
  258.1 0.0 copy-start.5
  258.1 56.5 %all-gather.2.cloned.1.call-done = f32[4608,192]{1,0:T(8,128)} async-done(((f32[1152,192]{1,0:T(8,128)}), f32[4608,192]{1,0:T(8,128)}) %all-gather.2.cloned.1.call-update) | async-done | bytes 3538960 | tf_op jit(solution)/shard_map/all_gather | solution.py:72
  314.7 3.9 copy.59
  318.5 19.1 %fusion.14 = f32[2,96,24,2,192,1]{4,1,2,0,3,5:T(8,128)S(1)} fusion(f32[1,96,2,192]{3,1,2,0:T(8,128)S(1)} %get-tuple-element.11, f32[1,96,2,192]{3,1,2,0:T(8,128)S(1)} %get-tuple-element.10, f32[2,192,2,24,192,1]{4,1,5,3,2,0:T(8,128)} %get-tuple-element.21, f32[192,24,192]{2,0,1:T(8,128)S(1)} %copy.59), kind=kOutput, calls=%fused_computation.17 | convolution fusion | flops 8157339648 | bytes 25067520 | tf_op jit(solution)/shard_map/bxzcy,okcx->bkzoy/dot_general | solution.py:40
  337.7 0.0 copy-done.4
  337.7 0.0 copy-done.5
  337.7 12.3 %fusion.5 = f32[2,96,24,2,96,1]{1,4,5,3,2,0:T(8,128)} fusion(f32[2,96,24,2,192,1]{4,1,2,0,3,5:T(8,128)S(1)} %fusion.14, f32[1,96,2,192]{3,1,2,0:T(8,128)S(1)} %get-tuple-element.11, f32[1,96,2,192]{3,1,2,0:T(8,128)S(1)} %get-tuple-element.10), kind=kOutput, calls=%fused_computation.7 | convolution fusion | flops 4076937216 | bytes 10911744 | tf_op jit(solution)/shard_map/bkzcy,ogcy->bkzog/dot_general | solution.py:40
  350.0 6.9 %copy.63 = f32[2,96,24,192]{3,2,0,1:T(8,128)} copy(f32[2,96,24,192]{1,3,2,0:T(8,128)} %bitcast.109) | data formatting | bytes 7077888 | tf_op jit(solution)/shard_map/reshape | solution.py:76
  356.9 4.9 all-to-all-start.1
  361.8 0.1 broadcast_add_fusion
  361.9 0.2 add_multiply_fusion
  362.1 104.9 %all-to-all-done.1 = f32[2,96,24,192]{3,2,0,1:T(8,128)} async-done(((f32[2,96,24,192]{3,2,0,1:T(8,128)}), f32[2,96,24,192]{3,2,0,1:T(8,128)}, u32[]{:S(2)}, u32[]{:S(2)}) %all-to-all-start.1) | async-done | bytes 3538976 | tf_op jit(solution)/shard_map/all_to_all | solution.py:79
  467.0 5.1 %copy.65 = f32[2,12,8,24,192]{4,3,2,1,0:T(8,128)} copy(f32[2,12,8,24,192]{4,3,0,1,2:T(8,128)} %bitcast.41) | data formatting | bytes 7077888 | tf_op jit(solution)/shard_map/all_to_all | solution.py:79
  472.1 0.0 copy-start.1
  472.1 0.0 copy-start.3
  472.1 7.3 %reshape.337 = f32[2,12,192,2,96]{4,3,2,1,0:T(2,128)} reshape(f32[2,12,8,24,192]{4,3,2,1,0:T(8,128)} %copy.65) | data formatting | bytes 7077888 | tf_op jit(solution)/shard_map/reshape | solution.py:80
  479.4 0.0 copy-done.1
  479.4 0.0 copy-done.3
  479.4 11.9 %fusion.17 = f32[2,12,96,2,96]{4,2,3,1,0:T(8,128)} fusion(f32[2,12,96,2,96]{4,2,3,1,0:T(8,128)S(1)} %copy-done.1, f32[2,12,192,2,96,1]{4,3,2,1,0,5:T(2,128)} %bitcast.114, f32[12,96,96]{2,1,0:T(8,128)S(1)} %add_multiply_fusion, f32[12,96,96]{2,1,0:T(8,128)S(1)} %copy-done.3, f32[1,96,2,192]{3,1,2,0:T(8,128)} %copy-done.5, f32[1,96,2,192]{3,1,2,0:T(8,128)} %copy-done.4), kind=kOutput, calls=%fused_computation.19 | convolution fusion | flops 2040274944 | bytes 8257536 | tf_op jit(solution)/shard_map/bxncg,ohcn->bxgoh/dot_general | solution.py:40
  491.3 2.0 copy.67
  493.4 2.1 copy.68
  495.5 4.8 copy.109
  (7 shorter events, 0.1 us)
Async XLA Ops:
  7.6 5.2 %copy-start.6 = (s32[12,96]{1,0:T(8,128)S(1)}, s32[12,96]{1,0:T(8,128)}, u32[]{:S(2)}) copy-start(s32[12,96]{1,0:T(8,128)} %param.6) | copy-start | bytes 13828
  12.8 7.9 %copy-start = (f32[2,12,96,2,96]{4,2,3,1,0:T(8,128)}, f32[2,12,96,2,96]{4,2,3,1,0:T(8,128)S(1)}, u32[]{:S(2)}) copy-start(f32[2,12,96,2,96]{4,2,3,1,0:T(8,128)S(1)} %copy.52) | copy-start | bytes 5308420
  13.1 1.0 copy-start.2
  28.7 6.7 %copy-start.7 = (s32[2]{0:T(128)S(1)}, s32[2]{0:T(128)}, u32[]{:S(2)}) copy-start(s32[2]{0:T(128)} %param.5) | copy-start | bytes 28
  28.7 111.8 %all-to-all-start = ((f32[2,12,192,192]{3,0,1,2:T(2,128)}), f32[2,12,192,192]{3,0,1,2:T(2,128)}, u32[]{:S(2)}, u32[]{:S(2)}) async-start(f32[2,12,192,192]{3,0,1,2:T(2,128)} %copy.54), calls=%async_computation | async-start | bytes 9437184 | tf_op jit(solution)/shard_map/all_to_all | solution.py:57
  35.2 218.8 %reduce-scatter.2.cloned.1.call-start = ((), (), s32[]{:S(2)}) async-start(), calls=%async_computation.3 | async-start | bytes 5898240 | tf_op jit(solution)/shard_map/reduce_scatter | solution.py:67
  197.9 116.8 %all-gather.2.cloned.1.call-start = ((), (), s32[]{:S(2)}) async-start(), calls=%async_computation.4 | async-start | bytes 5898240 | tf_op jit(solution)/shard_map/all_gather | solution.py:72
  258.1 79.5 %copy-start.4 = (f32[1,96,2,192]{3,1,2,0:T(8,128)}, f32[1,96,2,192]{3,1,2,0:T(8,128)S(1)}, u32[]{:S(2)}) copy-start(f32[1,96,2,192]{3,1,2,0:T(8,128)S(1)} %get-tuple-element.10) | copy-start | bytes 442372
  258.1 79.5 %copy-start.5 = (f32[1,96,2,192]{3,1,2,0:T(8,128)}, f32[1,96,2,192]{3,1,2,0:T(8,128)S(1)}, u32[]{:S(2)}) copy-start(f32[1,96,2,192]{3,1,2,0:T(8,128)S(1)} %get-tuple-element.11) | copy-start | bytes 442372
  356.9 110.1 %all-to-all-start.1 = ((f32[2,96,24,192]{3,2,0,1:T(8,128)}), f32[2,96,24,192]{3,2,0,1:T(8,128)}, u32[]{:S(2)}, u32[]{:S(2)}) async-start(f32[2,96,24,192]{3,2,0,1:T(8,128)} %copy.63), calls=%async_computation.2 | async-start | bytes 9437184 | tf_op jit(solution)/shard_map/all_to_all | solution.py:79
  472.1 7.3 %copy-start.1 = (f32[2,12,96,2,96]{4,2,3,1,0:T(8,128)S(1)}, f32[2,12,96,2,96]{4,2,3,1,0:T(8,128)}, u32[]{:S(2)}) copy-start(f32[2,12,96,2,96]{4,2,3,1,0:T(8,128)} %copy-done) | copy-start | bytes 5308420
  472.1 7.3 %copy-start.3 = (f32[12,96,96]{2,1,0:T(8,128)S(1)}, f32[12,96,96]{2,1,0:T(8,128)}, u32[]{:S(2)}) copy-start(f32[12,96,96]{2,1,0:T(8,128)} %copy-done.2) | copy-start | bytes 1327108
Sparse Core Ops, SparseCore 0:
  198.0 55.9 reduce-scatter.1
  257.7 56.9 all-gather.1
where the time goes:
time: 513 us; the launch traced here: 507 us
  waiting for transfers between devices  323 us (63%)
  matrix products  81 us (16%)
  local copies, waits for them, and re-layouts  68.2 us (13%)
  between operations  14.5 us (3%)
  starting transfers between devices  11.6 us (2%)
  other arithmetic  9.57 us (2%)
    all_to_all x1, waiting for transfers between devices, shards(): lax.all_to_all(flattened, 'slab', split_axis=2, concat_axis=1, tiled=True)  105 us
    all_to_all x1, waiting for transfers between devices, shards(): lax.all_to_all(back_y, 'slab', split_axis=1, concat_axis=2, tiled=True)  105 us
    dot_general x6, matrix products, contract(): return jnp.einsum(form, left, right, precision=lax.Precision.HIGHEST)  81 us
    all_gather x1, waiting for transfers between devices, shards(): gathered = lax.all_gather(own_potential, 'band', axis=0, tiled=True)  56.5 us
    reduce_scatter x1, waiting for transfers between devices, shards(): lax.psum_scatter(flat_partial, 'band', scatter_dimension=0, tiled=True)  56 us
    unnamed x19, local copies, waits for them, and re-layouts  11.1 us
  transfers between devices with their start and end apart: 4, of which 4 were waited for; matrix products, arithmetic and copies ran while one was open for 0% of the time, Pallas kernels for 0%

commit v1 on v0

--- a/solution.py
+++ b/solution.py
@@ -2,11 +2,13 @@
 
 import jax
 import jax.numpy as jnp
+import numpy as np
 from jax import lax
 from jax.sharding import PartitionSpec as P
 
 KINETIC = 0.0005
 SLATER = 0.9847
+PARTS = 3
 
 
 def frequency(length):
@@ -37,10 +39,10 @@
 
 
 def contract(form, left, right):
-    return jnp.einsum(form, left, right, precision=lax.Precision.HIGHEST)
-
-
-def shards(coefficients, occupation, pencil_reach, external):
+    return jnp.einsum(form, left, right, precision=lax.Precision.HIGH)
+
+
+def slab_plan(coefficients, occupation, pencil_reach, external):
     nbands, planes, width, doubled = coefficients.shape
     points = 2 * width
     slabs = lax.axis_size("slab")
@@ -88,6 +90,125 @@
     return (finished.reshape(nbands, planes, width, 2 * width), potential_all)
 
 
+def tables(length, extent):
+    indices = np.arange(length)
+    wavenumbers = np.where(indices < length // 2, indices, indices - length)
+    angles = (np.arange(extent)[:, None] * wavenumbers[None, :] % extent) * (2.0 * math.pi / extent)
+    cosine, sine = np.cos(angles), np.sin(angles)
+    inverse = np.stack([np.stack([cosine, -sine], 1), np.stack([sine, cosine], 1)], 0) * length ** -0.5
+    cosine, sine = cosine.T, sine.T
+    forward = np.stack([np.stack([cosine, sine], 1), np.stack([-sine, cosine], 1)], 0) * (length**0.5 / extent)
+    return inverse.astype(np.float32), forward.astype(np.float32)
+
+
+def exchange_plan(coefficients, occupation, pencil_reach, external, parts):
+    nbands, planes, width, doubled = coefficients.shape
+    points = 2 * width
+    slabs = lax.axis_size("slab")
+    groups = lax.axis_size("band")
+    layers = points // slabs
+    own = layers // groups
+    count = own // parts
+    everyone = ("band", "slab")
+    members = groups * slabs
+    group = lax.axis_index("band")
+    inverse, forward = tables(width, points)
+    wavenumbers = frequency(width)
+    sphere = (jnp.abs(wavenumbers)[None, None, :] <= pencil_reach[:, :, None]).astype(jnp.float32)
+    sphere_full = jnp.concatenate([sphere, sphere], 2)[None]
+    masked = coefficients * sphere_full
+    rows = masked.reshape(nbands * planes * width, doubled)
+
+    inverse_z = inverse.reshape(2, slabs, groups, parts, count, 2, width).transpose(3, 2, 1, 4, 0, 5, 6)
+    inverse_z = inverse_z.reshape(parts, members * count * 2, doubled)
+    forward_z = forward.reshape(2, width, 2, slabs, groups, parts, count).transpose(5, 4, 3, 6, 2, 0, 1)
+    forward_z = forward_z.reshape(parts, members * count * 2, doubled)
+
+    def swaps(shift):
+        if groups & (groups - 1) == 0:
+            return [(source, source ^ shift) for source in range(groups)], group ^ shift
+        return [(source, (source + shift) % groups) for source in range(groups)], (group - shift) % groups
+
+    def around(value):
+        found = {0: value}
+        for shift in range(1, groups):
+            found[shift] = lax.ppermute(value, "band", swaps(shift)[0])
+        origins = {shift: swaps(shift)[1] for shift in found}
+        whole = []
+        for member in range(groups):
+            chosen = value
+            for shift in range(1, groups):
+                chosen = jnp.where(origins[shift] == member, found[shift], chosen)
+            whole.append(chosen)
+        return jnp.stack(whole)
+
+    weights = around(occupation.astype(jnp.float32) / (nbands * groups)).reshape(-1)
+    own_external = lax.dynamic_slice_in_dim(external, group * own, own, 1)
+
+    def spread_out(along_z):
+        return lax.all_to_all(along_z.reshape(members, count * 2, rows.shape[0]), everyone, 0, 0, tiled=True)
+
+    def transform(part, current):
+        current = current.reshape(groups, slabs, count, 2, nbands, planes, width)
+        spread = contract("gszcbkw,oycw->zgbskoy", current, inverse)
+        spread = spread.reshape(count, groups * nbands, slabs * planes, 2, points)
+        wavefield = contract("zbkcy,oxck->zboxy", spread, inverse)
+        density = jnp.sum(weights[None, :, None, None] * jnp.sum(wavefield * wavefield, 2), 1)
+        potential = own_external[:, part * count:(part + 1) * count].transpose(1, 0, 2) - SLATER * jnp.cbrt(density)
+        product = wavefield * potential[:, None, None]
+        back_x = contract("zbcxy,okcx->zbkoy", product, forward)
+        back_y = contract("zbkcy,owcy->zbkow", back_x, forward)
+        back_y = back_y.reshape(count, groups, nbands, slabs, planes, 2, width).transpose(1, 3, 0, 5, 2, 4, 6)
+        return back_y.reshape(members, count * 2, rows.shape[0]), potential
+
+    def gather_back(block):
+        return lax.all_to_all(block, everyone, 0, 0, tiled=True)
+
+    def finish(part, block):
+        return contract("rn,rk->nk", block.reshape(members * count * 2, rows.shape[0]), forward_z[part])
+
+    def after(value, *earlier):
+        corner = (0,) * value.ndim
+        marks = [(other[(0,) * other.ndim] > 3e38).astype(value.dtype) for other in earlier]
+        return value.at[corner].add(sum(marks))
+
+    worked = []
+    arriving = spread_out(contract("rk,nk->rn", inverse_z[0], rows))
+    for part in range(parts):
+        arrived = arriving
+        if part + 1 < parts:
+            outgoing = contract("rk,nk->rn", inverse_z[part + 1], rows)
+            arriving = spread_out(after(outgoing, worked[-1][0]) if worked else outgoing)
+        worked.append(transform(part, arrived))
+    returned = 0.0
+    for part in range(parts):
+        block = worked[part][0]
+        if part + 2 < parts:
+            block = after(block, worked[part + 1][0])
+        returned = returned + finish(part, gather_back(block))
+    own_potential = jnp.concatenate([potential for _, potential in worked], 0)
+    gathered = lax.all_gather(own_potential, "band", axis=0, tiled=True)
+    potential_all = gathered.transpose(1, 0, 2)
+    plane_index = lax.axis_index("slab") * planes + jnp.arange(planes, dtype=jnp.int32)
+    plane_freq = jnp.where(plane_index < width // 2, plane_index, plane_index - width)
+    plane_sq = (plane_freq * plane_freq).astype(jnp.float32)
+    wave_sq = (wavenumbers * wavenumbers).astype(jnp.float32)
+    twice_sq = jnp.concatenate([wave_sq, wave_sq])
+    kinetic = KINETIC * (plane_sq[:, None, None] + wave_sq[None, :, None] + twice_sq[None, None, :])
+    finished = sphere_full * (kinetic[None] * masked + returned.reshape(masked.shape))
+    return (finished, potential_all)
+
+
+def shards(*operands):
+    layers = 2 * operands[0].shape[2] // lax.axis_size("slab")
+    groups = lax.axis_size("band")
+    if layers % groups == 0:
+        own = layers // groups
+        parts = next(p for p in (PARTS, 2, 3, 1) if own % p == 0)
+        return exchange_plan(*operands, parts)
+    return slab_plan(*operands)
+
+
 def solution(mesh):
     return jax.shard_map(
         shards,

time: 513 us -> 290 us (0.57)
  waiting for transfers between devices: 323 us -> 98.6 us
  matrix products: 81 us -> 62 us
  starting transfers between devices: 11.6 us -> 29.9 us
    all_to_all x2 -> x6, waiting for transfers between devices: 210 us -> 98.5 us  [the longest x3 68.6 us: gather_back(): return lax.all_to_all(block, everyone, 0, 0, tiled=True)]
    all_gather x1, waiting for transfers between devices: 56.5 us -> 0.01 us  [exchange_plan(): gathered = lax.all_gather(own_potential, 'band', axis=0, tiled=True)]
    reduce_scatter x1 -> x0, waiting for transfers between devices: 56 us -> none  [shards(): lax.psum_scatter(flat_partial, 'band', scatter_dimension=0, tiled=True)]
    dot_general x6 -> x18, matrix products: 81 us -> 62 us  [contract(): return jnp.einsum(form, left, right, precision=lax.Precision.HIGH)]
    all_to_all x2 -> x6, starting transfers between devices: 11.4 us -> 26.3 us  [the longest x3 17 us: spread_out(): lax.all_to_all(along_z.reshape(members, count * 2, rows.shape[0]), everyo...]
    all_to_all x3 -> x0, local copies, waits for them, and re-layouts: 11.7 us -> none  [the longest x2 6.57 us: shards(): lax.all_to_all(flattened, 'slab', split_axis=2, concat_axis=1, tiled=True)]
    reshape x5 -> x14, local copies, waits for them, and re-layouts: 31.3 us -> 23.3 us  [the longest x5 7.45 us: transform(): return (back_y.reshape(members, count * 2, rows.shape[0]), potential)]
    transpose x1 -> x4, local copies, waits for them, and re-layouts: 2.72 us -> 9.69 us  [the longest x3 9.18 us: contract(): return jnp.einsum(form, left, right, precision=lax.Precision.HIGH)]
  transfers between devices with their start and end apart: 4 -> 10, of which waited for: 4 -> 5; matrix products, arithmetic and copies ran while one was open for 0% -> 34% of each run, Pallas kernels for 0% -> 0%
where the time goes in v1:
time: 290 us; the launch traced here: 284 us
  waiting for transfers between devices  98.6 us (34%)
  local copies, waits for them, and re-layouts  64.5 us (22%)
  matrix products  62 us (21%)
  starting transfers between devices  29.9 us (10%)
  between operations  17.4 us (6%)
  other arithmetic  12 us (4%)
    all_to_all x3, waiting for transfers between devices, gather_back(): return lax.all_to_all(block, everyone, 0, 0, tiled=True)  68.6 us
    dot_general x18, matrix products, contract(): return jnp.einsum(form, left, right, precision=lax.Precision.HIGH)  62 us
    all_to_all x3, waiting for transfers between devices, spread_out(): lax.all_to_all(along_z.reshape(members, count * 2, rows.shape[0]), everyo...  30 us
    all_to_all x3, starting transfers between devices, spread_out(): lax.all_to_all(along_z.reshape(members, count * 2, rows.shape[0]), everyo...  17 us
    unnamed x54, local copies, waits for them, and re-layouts  11.6 us
    all_to_all x3, starting transfers between devices, gather_back(): return lax.all_to_all(block, everyone, 0, 0, tiled=True)  9.28 us
    transpose x3, local copies, waits for them, and re-layouts, contract(): return jnp.einsum(form, left, right, precision=lax.Precision.HIGH)  9.18 us
    reshape x5, local copies, waits for them, and re-layouts, transform(): return (back_y.reshape(members, count * 2, rows.shape[0]), potential)  7.45 us
  transfers between devices with their start and end apart: 10, of which 5 were waited for; matrix products, arithmetic and copies ran while one was open for 34% of the time, Pallas kernels for 0%

profile of v1, /device:TPU:0, one launch (start us, length us, event | category | flops | bytes accessed | tf_op | source)
XLA Modules:
  0.0 284.3 jit_solution(14449870398646658848)
XLA Ops:
  7.2 0.9 broadcast_compare_fusion
  8.5 2.4 broadcast_multiply_fusion
  10.9 1.3 fusion.43
  12.2 1.4 reshape.205
  13.6 7.3 %all-to-all-start = ((f32[32,4,2304]{2,1,0:T(4,128)}), f32[32,4,2304]{2,1,0:T(4,128)S(1)}, u32[]{:S(2)}, u32[]{:S(2)}) async-start(f32[32,4,2304]{2,1,0:T(4,128)} %reshape.205), calls=%async_computation | async-start | bytes 2359296 | tf_op jit(solution)/shard_map/all_to_all | solution.py:149
  21.5 2.7 collective-permute-start
  25.0 3.2 %fusion.44 = f32[128,2304]{1,0:T(8,128)} fusion(f32[128,192]{1,0:T(8,128)} %constant.114.clone, f32[2304,192]{1,0:T(8,128)S(1)} %bitcast.196), kind=kOutput, calls=%fused_computation.83 | convolution fusion | flops 339738624 | bytes 3047424 | tf_op jit(solution)/shard_map/rk,nk->rn/dot_general | solution.py:42
  28.2 2.6 reshape.210
  30.9 3.0 %fusion.46 = f32[2304,128]{1,0:T(8,128)} fusion(f32[2304,192]{1,0:T(8,128)S(1)} %bitcast.197, f32[128,192]{1,0:T(8,128)} %constant.117.clone), kind=kOutput, calls=%fused_computation.85 | convolution fusion | flops 339738624 | bytes 3047424 | tf_op jit(solution)/shard_map/rk,nk->rn/dot_general | solution.py:42
  33.9 17.3 %all-to-all-done = f32[32,4,2304]{2,1,0:T(4,128)S(1)} async-done(((f32[32,4,2304]{2,1,0:T(4,128)}), f32[32,4,2304]{2,1,0:T(4,128)S(1)}, u32[]{:S(2)}, u32[]{:S(2)}) %all-to-all-start) | async-done | bytes 1179680 | tf_op jit(solution)/shard_map/all_to_all | solution.py:149
  51.2 3.6 %all-to-all-start.1 = ((f32[32,4,2304]{2,1,0:T(4,128)}), f32[32,4,2304]{2,1,0:T(4,128)}, u32[]{:S(2)}, u32[]{:S(2)}) async-start(f32[32,4,2304]{2,1,0:T(4,128)} %reshape.210), calls=%async_computation.1 | async-start | bytes 2359296 | tf_op jit(solution)/shard_map/all_to_all | solution.py:149
  54.7 4.1 %constant_dynamic-slice_fusion.2 = (f32[192,2,192]{2,1,0:T(2,128)}, f32[192,2,192]{2,1,0:T(2,128)}, f32[192,2,192]{2,1,0:T(2,128)S(1)}) fusion(f32[192,24,192]{2,1,0:T(8,128)} %param.29, s32[]{:T(128)S(6)} %add.101, s32[]{:T(128)S(6)} %add.100, s32[]{:T(128)S(6)} %select_n.105), kind=kLoop, calls=%fused_computation.72 | loop fusion | bytes 1769484 | tf_op jit(solution)/shard_map/slice | solution.py:157
  58.8 0.9 copy.215
  59.8 1.2 slice.64
  61.1 1.2 reshape.253
  62.4 2.9 %convolution_bitcast_fusion.2 = f32[2,4,2,8,12,2,192]{6,4,5,2,0,3,1:T(8,128)S(1)} fusion(f32[2,192,2,96,1,1,1,1]{3,1,2,0,7,6,5,4:T(8,128)} %constant.124, f32[4,8,2,2,2,12,96]{6,5,4,3,2,1,0:T(8,128)S(1)} %reshape.253), kind=kOutput, calls=%fused_computation.38 | convolution fusion | flops 679477248 | bytes 3833856 | tf_op jit(solution)/shard_map/gszcbkw,oycw->zgbskoy/dot_general | solution.py:42
  65.3 3.1 %copy.128 = f32[2,4,2,8,12,2,192]{6,5,4,3,2,1,0:T(2,128)S(1)} copy(f32[2,4,2,8,12,2,192]{6,4,5,2,0,3,1:T(8,128)S(1)} %convolution_bitcast_fusion.2) | data formatting | bytes 4718592 | tf_op jit(solution)/shard_map/gszcbkw,oycw->zgbskoy/transpose | solution.py:42
  68.4 6.5 %fusion.8 = (f32[2,8,192,192]{2,3,1,0:T(8,128)S(1)}, f32[2,8,192,2,192,1]{4,2,5,3,1,0:T(8,128)S(1)}) fusion(f32[2,192,2,96,1,1]{3,1,2,0,5,4:T(8,128)S(1)} %copy-done.6, f32[2,8,96,2,192,1]{4,3,2,1,0,5:T(2,128)S(1)} %bitcast.199), kind=kOutput, calls=%fused_computation.14 | convolution fusion | flops 1360723968 | bytes 9732096 | tf_op jit(solution)/shard_map/zbkcy,oxck->zboxy/dot_general | solution.py:42
  76.2 2.9 %fusion.4 = f32[2,8,192,2,96,1]{4,2,5,3,1,0:T(8,128)S(1)} fusion(f32[2,96,2,192,1,1]{3,1,2,0,5,4:T(8,128)S(1)} %copy-done, f32[2,8,192,2,192,1]{4,2,5,3,1,0:T(8,128)S(1)} %get-tuple-element.40, f32[2,192,192]{1,2,0:T(8,128)S(1)} %bitcast_subtract_fusion.2), kind=kOutput, calls=%fused_computation.4 | convolution fusion | flops 1360134144 | bytes 7667712 | tf_op jit(solution)/shard_map/zbcxy,okcx->zbkoy/dot_general | solution.py:42
  79.2 3.1 %fusion.27 = f32[2,8,96,2,96]{4,2,3,1,0:T(8,128)S(1)} fusion(f32[2,96,2,192,1,1]{3,1,2,0,5,4:T(8,128)S(1)} %copy-done, f32[2,8,192,2,96,1]{4,2,5,3,1,0:T(8,128)S(1)} %fusion.4), kind=kOutput, calls=%fused_computation.42 | convolution fusion | flops 679477248 | bytes 3833856 | tf_op jit(solution)/shard_map/zbkcy,owcy->zbkow/dot_general | solution.py:42
  82.3 0.9 copy.132
  83.8 2.0 reshape.209
  85.7 1.3 slice.62
  88.3 1.3 scatter-add.9
  89.6 1.6 copy.147
  91.2 1.4 reshape.218
  92.6 6.2 %all-to-all-start.4 = ((f32[32,4,2304]{2,1,0:T(4,128)}), f32[32,4,2304]{2,1,0:T(4,128)}, u32[]{:S(2)}, u32[]{:S(2)}) async-start(f32[32,4,2304]{2,1,0:T(4,128)} %reshape.218), calls=%async_computation.4 | async-start | bytes 2359296 | tf_op jit(solution)/shard_map/all_to_all | solution.py:149
  98.8 0.9 copy.217
  99.7 1.0 copy.218
  100.7 2.4 reshape.254
  103.1 1.9 convolution_bitcast_fusion.1
  105.0 3.1 %copy.137 = f32[2,4,2,8,12,2,192]{6,5,4,3,2,1,0:T(2,128)S(1)} copy(f32[2,4,2,8,12,2,192]{6,4,5,2,0,3,1:T(8,128)S(1)} %convolution_bitcast_fusion.1) | data formatting | bytes 4718592 | tf_op jit(solution)/shard_map/gszcbkw,oycw->zgbskoy/transpose | solution.py:42
  108.1 8.2 %fusion.7 = (f32[2,8,192,192]{2,3,1,0:T(8,128)S(1)}, f32[2,8,192,2,192,1]{4,2,5,3,1,0:T(8,128)}) fusion(f32[2,192,2,96,1,1]{3,1,2,0,5,4:T(8,128)S(1)} %copy-done.7, f32[2,8,96,2,192,1]{4,3,2,1,0,5:T(2,128)S(1)} %bitcast.200), kind=kOutput, calls=%fused_computation.11 | convolution fusion | flops 1360723968 | bytes 9732096 | tf_op jit(solution)/shard_map/zbkcy,oxck->zboxy/dot_general | solution.py:42
  116.3 12.7 %all-to-all-done.4 = f32[32,4,2304]{2,1,0:T(4,128)} async-done(((f32[32,4,2304]{2,1,0:T(4,128)}), f32[32,4,2304]{2,1,0:T(4,128)}, u32[]{:S(2)}, u32[]{:S(2)}) %all-to-all-start.4) | async-done | bytes 1179680 | tf_op jit(solution)/shard_map/all_to_all | solution.py:149
  129.0 3.4 %reshape.255 = f32[4,8,2,2,2,12,96]{6,5,4,3,2,1,0:T(8,128)} reshape(f32[32,4,2304]{2,1,0:T(4,128)} %all-to-all-done.4) | data formatting | bytes 2359296 | tf_op jit(solution)/shard_map/reshape | solution.py:152
  132.4 3.5 %convolution_bitcast_fusion = f32[2,4,2,8,12,2,192]{6,4,5,2,0,3,1:T(8,128)S(1)} fusion(f32[2,192,2,96,1,1,1,1]{3,1,2,0,7,6,5,4:T(8,128)} %constant.124, f32[4,8,2,2,2,12,96]{6,5,4,3,2,1,0:T(8,128)} %reshape.255), kind=kOutput, calls=%fused_computation.36 | convolution fusion | flops 679477248 | bytes 3833856 | tf_op jit(solution)/shard_map/gszcbkw,oycw->zgbskoy/dot_general | solution.py:42
  136.0 3.1 %copy.150 = f32[2,4,2,8,12,2,192]{6,5,4,3,2,1,0:T(2,128)S(1)} copy(f32[2,4,2,8,12,2,192]{6,4,5,2,0,3,1:T(8,128)S(1)} %convolution_bitcast_fusion) | data formatting | bytes 4718592 | tf_op jit(solution)/shard_map/gszcbkw,oycw->zgbskoy/transpose | solution.py:42
  139.0 6.3 %fusion.6 = (f32[2,8,192,192]{2,3,1,0:T(8,128)S(1)}, f32[2,8,192,2,192,1]{4,2,5,3,1,0:T(8,128)S(1)}) fusion(f32[2,192,2,96,1,1]{3,1,2,0,5,4:T(8,128)S(1)} %copy-done.8, f32[2,8,96,2,192,1]{4,3,2,1,0,5:T(2,128)S(1)} %bitcast.198), kind=kOutput, calls=%fused_computation.8 | convolution fusion | flops 1360723968 | bytes 9732096 | tf_op jit(solution)/shard_map/zbkcy,oxck->zboxy/dot_general | solution.py:42
  146.5 0.9 bitcast_subtract_fusion
  147.4 2.9 %fusion = f32[2,8,192,2,96,1]{4,2,5,3,1,0:T(8,128)S(1)} fusion(f32[2,96,2,192,1,1]{3,1,2,0,5,4:T(8,128)S(1)} %copy-done, f32[2,8,192,2,192,1]{4,2,5,3,1,0:T(8,128)S(1)} %get-tuple-element.42, f32[2,192,192]{1,2,0:T(8,128)S(1)} %get-tuple-element.45), kind=kOutput, calls=%fused_computation | convolution fusion | flops 1360134144 | bytes 7667712 | tf_op jit(solution)/shard_map/zbcxy,okcx->zbkoy/dot_general | solution.py:42
  150.3 3.1 %fusion.33 = f32[2,8,96,2,96]{4,2,3,1,0:T(8,128)S(1)} fusion(f32[2,96,2,192,1,1]{3,1,2,0,5,4:T(8,128)S(1)} %copy-done, f32[2,8,192,2,96,1]{4,2,5,3,1,0:T(8,128)S(1)} %fusion), kind=kOutput, calls=%fused_computation.44 | convolution fusion | flops 679477248 | bytes 3833856 | tf_op jit(solution)/shard_map/zbkcy,owcy->zbkow/dot_general | solution.py:42
  153.5 0.9 copy.153
  154.9 2.2 reshape.256
  157.1 3.8 %all-to-all-start.5 = ((f32[32,4,2304]{2,1,0:T(4,128)}), f32[32,4,2304]{2,1,0:T(4,128)}, u32[]{:S(2)}, u32[]{:S(2)}) async-start(f32[32,4,2304]{2,1,0:T(4,128)} %reshape.256), calls=%async_computation.5 | async-start | bytes 2359296 | tf_op jit(solution)/shard_map/all_to_all | solution.py:165
  160.9 4.9 %fusion.2 = f32[2,8,192,2,96,1]{4,2,5,3,1,0:T(8,128)S(1)} fusion(f32[2,96,2,192,1,1]{3,1,2,0,5,4:T(8,128)S(1)} %copy-done, f32[2,8,192,2,192,1]{4,2,5,3,1,0:T(8,128)} %get-tuple-element.44, f32[2,192,192]{1,2,0:T(8,128)S(1)} %get-tuple-element.46), kind=kOutput, calls=%fused_computation.2 | convolution fusion | flops 1360134144 | bytes 7667712 | tf_op jit(solution)/shard_map/zbcxy,okcx->zbkoy/dot_general | solution.py:42
  165.8 3.1 %fusion.30 = f32[2,8,96,2,96]{4,2,3,1,0:T(8,128)S(1)} fusion(f32[2,96,2,192,1,1]{3,1,2,0,5,4:T(8,128)S(1)} %copy-done, f32[2,8,192,2,96,1]{4,2,5,3,1,0:T(8,128)S(1)} %fusion.2), kind=kOutput, calls=%fused_computation.43 | convolution fusion | flops 679477248 | bytes 3833856 | tf_op jit(solution)/shard_map/zbkcy,owcy->zbkow/dot_general | solution.py:42
  169.0 0.9 copy.140
  170.5 2.2 reshape.257
  172.7 1.2 slice.63
  175.2 1.8 copy.144
  177.0 14.2 %all-to-all-done.5 = f32[32,4,2304]{2,1,0:T(4,128)} async-done(((f32[32,4,2304]{2,1,0:T(4,128)}), f32[32,4,2304]{2,1,0:T(4,128)}, u32[]{:S(2)}, u32[]{:S(2)}) %all-to-all-start.5) | async-done | bytes 1179680 | tf_op jit(solution)/shard_map/all_to_all | solution.py:165
  191.2 2.7 all-to-all-start.2
  194.1 1.5 copy.157
  195.6 28.5 %all-to-all-done.2 = f32[32,4,2304]{2,1,0:T(4,128)S(1)} async-done(((f32[32,4,2304]{2,1,0:T(4,128)}), f32[32,4,2304]{2,1,0:T(4,128)S(1)}, u32[]{:S(2)}, u32[]{:S(2)}) %all-to-all-start.2) | async-done | bytes 1179680 | tf_op jit(solution)/shard_map/all_to_all | solution.py:165
  224.1 2.8 all-to-all-start.3
  227.2 1.2 add_multiply_fusion.1
  228.4 2.6 reshape.223
  231.4 25.8 %all-to-all-done.3 = f32[32,4,2304]{2,1,0:T(4,128)S(1)} async-done(((f32[32,4,2304]{2,1,0:T(4,128)}), f32[32,4,2304]{2,1,0:T(4,128)S(1)}, u32[]{:S(2)}, u32[]{:S(2)}) %all-to-all-start.3) | async-done | bytes 1179680 | tf_op jit(solution)/shard_map/all_to_all | solution.py:165
  257.7 1.8 fusion.45
  259.5 0.9 convolution_add_fusion.1
  260.8 2.1 convolution_add_fusion
  262.9 3.1 %copy.156 = f32[2304,192]{1,0:T(8,128)} copy(f32[2304,192]{0,1:T(8,128)} %convolution_add_fusion) | data formatting | bytes 3538944 | tf_op jit(solution)/shard_map/add | solution.py:188
  266.0 4.0 %add_multiply_fusion = f32[2,12,96,192]{3,2,1,0:T(8,128)} fusion(f32[2,12,96,192]{3,2,1,0:T(8,128)} %bitcast.201, f32[12,96,192]{2,1,0:T(8,128)} %add_multiply_fusion.1, f32[12,96,192]{2,1,0:T(8,128)S(1)} %copy-done.2, f32[2,12,96,192]{3,2,1,0:T(8,128)S(1)} %copy-done.3), kind=kLoop, calls=%fused_computation.35 | loop fusion | flops 1769472 | bytes 7077888 | tf_op jit(solution)/shard_map/mul | solution.py:198
  270.0 7.3 %copy.158 = f32[192,24,192]{2,1,0:T(8,128)} copy(f32[192,24,192]{2,0,1:T(8,128)} %bitcast.206) | data formatting | bytes 7077888
  (79 shorter events, 7.6 us)
Async XLA Ops:
  8.5 2.4 copy-start.1
  8.5 2.4 copy-start.23
  12.2 8.7 %copy-start.24 = (s32[2]{0:T(128)S(1)}, s32[2]{0:T(128)}, u32[]{:S(2)}) copy-start(s32[2]{0:T(128)} %param.27) | copy-start | bytes 28
  13.6 37.6 %all-to-all-start = ((f32[32,4,2304]{2,1,0:T(4,128)}), f32[32,4,2304]{2,1,0:T(4,128)S(1)}, u32[]{:S(2)}, u32[]{:S(2)}) async-start(f32[32,4,2304]{2,1,0:T(4,128)} %reshape.205), calls=%async_computation | async-start | bytes 2359296 | tf_op jit(solution)/shard_map/all_to_all | solution.py:149
  21.5 39.5 %collective-permute-start = (f32[2]{0:T(128)}, f32[2]{0:T(128)S(1)}, u32[]{:S(2)}, u32[]{:S(2)}) collective-permute-start(f32[2]{0:T(128)} %convert_multiply_fusion), channel_id=1, source_target_pairs={{0,24},{8,16},{16,8},{24,0},{1,25},{9,17},{17,9},{25,1},{2,26},{10... | collective-permute-start | bytes 32 | tf_op jit(solution)/shard_map/ppermute | solution.py:135
  24.2 36.8 %collective-permute-start.1 = (f32[2]{0:T(128)}, f32[2]{0:T(128)S(1)}, u32[]{:S(2)}, u32[]{:S(2)}) collective-permute-start(f32[2]{0:T(128)} %convert_multiply_fusion), channel_id=1, source_target_pairs={{0,16},{8,24},{16,0},{24,8},{1,17},{9,25},{17,1},{25,9},{2,18},{10... | collective-permute-start | bytes 32 | tf_op jit(solution)/shard_map/ppermute | solution.py:135
  24.7 36.3 %collective-permute-start.2 = (f32[2]{0:T(128)}, f32[2]{0:T(128)S(1)}, u32[]{:S(2)}, u32[]{:S(2)}) collective-permute-start(f32[2]{0:T(128)} %convert_multiply_fusion), channel_id=1, source_target_pairs={{0,8},{8,0},{16,24},{24,16},{1,9},{9,1},{17,25},{25,17},{2,10},{10... | collective-permute-start | bytes 32 | tf_op jit(solution)/shard_map/ppermute | solution.py:135
  51.2 41.4 %all-to-all-start.1 = ((f32[32,4,2304]{2,1,0:T(4,128)}), f32[32,4,2304]{2,1,0:T(4,128)}, u32[]{:S(2)}, u32[]{:S(2)}) async-start(f32[32,4,2304]{2,1,0:T(4,128)} %reshape.210), calls=%async_computation.1 | async-start | bytes 2359296 | tf_op jit(solution)/shard_map/all_to_all | solution.py:149
  65.3 3.1 %copy-start.6 = (f32[2,192,2,96,1,1]{3,1,2,0,5,4:T(8,128)S(1)}, f32[2,192,2,96,1,1]{3,1,2,0,5,4:T(8,128)}, u32[]{:S(2)}) copy-start(f32[2,192,2,96,1,1]{3,1,2,0,5,4:T(8,128)} %constant.125) | copy-start | bytes 884740
  74.9 1.0 copy-start.20
  74.9 1.3 copy-start
  76.2 3.0 %copy-start.13 = (f32[2,192,192]{1,2,0:T(8,128)}, f32[2,192,192]{1,2,0:T(8,128)S(1)}, u32[]{:S(2)}) copy-start(f32[2,192,192]{1,2,0:T(8,128)S(1)} %bitcast_subtract_fusion.2) | copy-start | bytes 884740
  91.2 7.5 %copy-start.17 = (f32[192,2,192]{2,1,0:T(2,128)S(1)}, f32[192,2,192]{2,1,0:T(2,128)}, u32[]{:S(2)}) copy-start(f32[192,2,192]{2,1,0:T(2,128)} %get-tuple-element.33) | copy-start | bytes 884740
  91.2 8.5 %copy-start.16 = (f32[192,2,192]{2,1,0:T(2,128)S(1)}, f32[192,2,192]{2,1,0:T(2,128)}, u32[]{:S(2)}) copy-start(f32[192,2,192]{2,1,0:T(2,128)} %get-tuple-element.32) | copy-start | bytes 884740
  92.6 36.4 %all-to-all-start.4 = ((f32[32,4,2304]{2,1,0:T(4,128)}), f32[32,4,2304]{2,1,0:T(4,128)}, u32[]{:S(2)}, u32[]{:S(2)}) async-start(f32[32,4,2304]{2,1,0:T(4,128)} %reshape.218), calls=%async_computation.4 | async-start | bytes 2359296 | tf_op jit(solution)/shard_map/all_to_all | solution.py:149
  98.7 4.4 %copy-start.15 = (f32[2,192,2,96,1,1,1,1]{3,1,2,0,7,6,5,4:T(8,128)S(1)}, f32[2,192,2,96,1,1,1,1]{3,1,2,0,7,6,5,4:T(8,128)}, u32[]{:S(2)}) copy-start(f32[2,192,2,96,1,1,1,1]{3,1,2,0,7,6,5,4:T(8,128)} %constant.124) | copy-start | bytes 884740
  105.0 3.1 %copy-start.7 = (f32[2,192,2,96,1,1]{3,1,2,0,5,4:T(8,128)S(1)}, f32[2,192,2,96,1,1]{3,1,2,0,5,4:T(8,128)}, u32[]{:S(2)}) copy-start(f32[2,192,2,96,1,1]{3,1,2,0,5,4:T(8,128)} %constant.125) | copy-start | bytes 884740
  135.9 3.1 %copy-start.8 = (f32[2,192,2,96,1,1]{3,1,2,0,5,4:T(8,128)S(1)}, f32[2,192,2,96,1,1]{3,1,2,0,5,4:T(8,128)}, u32[]{:S(2)}) copy-start(f32[2,192,2,96,1,1]{3,1,2,0,5,4:T(8,128)} %constant.125) | copy-start | bytes 884740
  145.4 1.0 copy-start.18
  145.4 1.1 copy-start.19
  147.3 3.0 %copy-start.9 = (f32[2,192,192]{1,2,0:T(8,128)}, f32[2,192,192]{1,2,0:T(8,128)S(1)}, u32[]{:S(2)}) copy-start(f32[2,192,192]{1,2,0:T(8,128)S(1)} %get-tuple-element.45) | copy-start | bytes 884740
  147.3 13.6 %copy-start.11 = (f32[2,192,192]{1,2,0:T(8,128)}, f32[2,192,192]{1,2,0:T(8,128)S(1)}, u32[]{:S(2)}) copy-start(f32[2,192,192]{1,2,0:T(8,128)S(1)} %get-tuple-element.46) | copy-start | bytes 884740
  157.1 34.1 %all-to-all-start.5 = ((f32[32,4,2304]{2,1,0:T(4,128)}), f32[32,4,2304]{2,1,0:T(4,128)}, u32[]{:S(2)}, u32[]{:S(2)}) async-start(f32[32,4,2304]{2,1,0:T(4,128)} %reshape.256), calls=%async_computation.5 | async-start | bytes 2359296 | tf_op jit(solution)/shard_map/all_to_all | solution.py:165
  170.5 4.7 %copy-start.4 = (f32[32,4,2304]{2,0,1:T(8,128)S(1)}, f32[32,4,2304]{2,0,1:T(8,128)}, u32[]{:S(2)}) copy-start(f32[32,4,2304]{2,0,1:T(8,128)} %reshape.209) | copy-start | bytes 3538948
  177.0 16.9 %copy-start.10 = (f32[2,192,192]{1,2,0:T(8,128)S(1)}, f32[2,192,192]{1,2,0:T(8,128)}, u32[]{:S(2)}) copy-start(f32[2,192,192]{1,2,0:T(8,128)} %copy-done.9) | copy-start | bytes 884740
  177.0 16.9 %copy-start.12 = (f32[2,192,192]{1,2,0:T(8,128)S(1)}, f32[2,192,192]{1,2,0:T(8,128)}, u32[]{:S(2)}) copy-start(f32[2,192,192]{1,2,0:T(8,128)} %copy-done.11) | copy-start | bytes 884740
  177.0 17.0 %copy-start.14 = (f32[2,192,192]{1,2,0:T(8,128)S(1)}, f32[2,192,192]{1,2,0:T(8,128)}, u32[]{:S(2)}) copy-start(f32[2,192,192]{1,2,0:T(8,128)} %copy-done.13) | copy-start | bytes 884740
  191.2 32.9 %all-to-all-start.2 = ((f32[32,4,2304]{2,1,0:T(4,128)}), f32[32,4,2304]{2,1,0:T(4,128)S(1)}, u32[]{:S(2)}, u32[]{:S(2)}) async-start(f32[32,4,2304]{2,1,0:T(4,128)} %copy.144), calls=%async_computation.2 | async-start | bytes 2359296 | tf_op jit(solution)/shard_map/all_to_all | solution.py:165
  193.9 76.1 %all-gather.2.cloned.1.call-start = ((), (), s32[]{:S(2)}) async-start(), calls=%async_computation.6 | async-start | bytes 5898240 | tf_op jit(solution)/shard_map/all_gather | solution.py:190
  224.1 33.1 %all-to-all-start.3 = ((f32[32,4,2304]{2,1,0:T(4,128)}), f32[32,4,2304]{2,1,0:T(4,128)S(1)}, u32[]{:S(2)}, u32[]{:S(2)}) async-start(f32[32,4,2304]{2,1,0:T(4,128)} %reshape.257), calls=%async_computation.3 | async-start | bytes 2359296 | tf_op jit(solution)/shard_map/all_to_all | solution.py:165
  257.7 1.9 copy-start.22
  259.5 1.3 copy-start.5
  259.5 1.3 copy-start.21
  262.9 3.1 %copy-start.2 = (f32[12,96,192]{2,1,0:T(8,128)S(1)}, f32[12,96,192]{2,1,0:T(8,128)}, u32[]{:S(2)}) copy-start(f32[12,96,192]{2,1,0:T(8,128)} %copy-done.1) | copy-start | bytes 2654212
  262.9 3.1 %copy-start.3 = (f32[2,12,96,192]{3,2,1,0:T(8,128)S(1)}, f32[2,12,96,192]{3,2,1,0:T(8,128)}, u32[]{:S(2)}) copy-start(f32[2,12,96,192]{3,2,1,0:T(8,128)} %param.26) | copy-start | bytes 5308420
Sparse Core Ops, SparseCore 0:
  196.5 71.4 all-gather.1
